TPU v7x, 128 devices: a whole 4x4x4 slice. The times are simulated.
128 devices in a mesh: section: 2 (over core), cin: 8 (over z_hi, y), cout: 8 (over z_lo, x).
Axes of the slice: x: 4, y: 4, z: 4 (z_hi: 2, z_lo: 2; z = z_hi * 2 + z_lo), core: 2. Of those that a mesh axis runs over, the one named last changes fastest.
Arguments:
- inner_features: bfloat16 [2, 784, 2560], P('section', None, ('cin', 'cout')), may hold values from 0 to 2
- block_input: bfloat16 [2, 784, 5120], P('section', None, ('cin', 'cout')), may hold values from -6 to 6
- first_kernel: bfloat16 [9, 2560, 2560], P(None, 'cin', 'cout'), may hold values from -0.0546875 to 0.0546875
- expand_weight: bfloat16 [2560, 5120], P('cout', 'cin'), may hold values from -0.15625 to 0.15625
- reduce_weight: bfloat16 [5120, 5120], P(('cin', 'section'), 'cout'), may hold values from -0.125 to 0.125
- stride_kernel: bfloat16 [9, 5120, 5120], P(None, 'cout', ('section', 'cin')), may hold values from -0.0390625 to 0.0390625
- output_grad: bfloat16 [2, 196, 5120], P(None, None, ('section', 'cin', 'cout')), may hold values from -6 to 6
Outputs:
- inner_gradient: float32 [2, 784, 2560], P('section', None, ('cin', 'cout'))
- input_gradient: bfloat16 [2, 784, 5120], P('section', None, ('cin', 'cout'))
- first_gradient: float32 [9, 2560, 2560], P(None, 'cin', 'cout')
- expand_gradient: float32 [2560, 5120], P('cout', 'cin')
- reduce_gradient: float32 [5120, 5120], P(('cin', 'section'), 'cout')
- stride_gradient: float32 [9, 5120, 5120], P(None, 'cout', ('section', 'cin'))
All inputs are finite; a program needn't handle non-finite values.
Results may differ from a plain program's by a relative error of at most 0.013.
Values may be sent and summed in bfloat16 or wider, within the bound.
A program may use at most 192 MiB of HBM per device.

v0:
```python
import jax
import jax.numpy as jnp
from jax import lax
from jax.sharding import PartitionSpec as P

SIDE = 28


def smooth_gate(values):
    return values * jax.nn.sigmoid(values)


def gate_slope(values):
    logistic = jax.nn.sigmoid(values)
    return logistic * (1.0 + values * (1.0 - logistic))


def flatten_rows(images):
    return images.reshape(images.shape[0] * images.shape[1], images.shape[2])


def project(images, matrix):
    product = jnp.dot(flatten_rows(images), matrix, preferred_element_type=jnp.float32)
    return product.reshape(images.shape[0], images.shape[1], matrix.shape[1])


def project_back(grads, matrix):
    product = lax.dot_general(
        flatten_rows(grads), matrix, (((1,), (1,)), ((), ())), preferred_element_type=jnp.float32
    )
    return product.reshape(grads.shape[0], grads.shape[1], matrix.shape[0])


def outer_rows(left, right):
    return lax.dot_general(
        flatten_rows(left),
        flatten_rows(right),
        (((0,), (0,)), ((), ())),
        preferred_element_type=jnp.float32,
    )


def padded_grid(images, side):
    grid = images.reshape(images.shape[0], side, side, images.shape[2])
    return jnp.pad(grid, ((0, 0), (1, 1), (1, 1), (0, 0)))


def conv_same(images, kernel, side):
    padded = padded_grid(images, side)
    total = jnp.zeros((images.shape[0] * side * side, kernel.shape[2]), jnp.float32)
    for row in range(3):
        for column in range(3):
            window = padded[:, row : row + side, column : column + side, :].reshape(
                -1, images.shape[2]
            )
            total = total + jnp.dot(
                window, kernel[3 * row + column], preferred_element_type=jnp.float32
            )
    return total.reshape(images.shape[0], side * side, kernel.shape[2])


def conv_same_back(grads, kernel, side):
    padded = padded_grid(grads, side)
    total = jnp.zeros((grads.shape[0] * side * side, kernel.shape[1]), jnp.float32)
    for row in range(3):
        for column in range(3):
            window = padded[:, 2 - row : 2 - row + side, 2 - column : 2 - column + side, :].reshape(
                -1, grads.shape[2]
            )
            total = total + lax.dot_general(
                window,
                kernel[3 * row + column],
                (((1,), (1,)), ((), ())),
                preferred_element_type=jnp.float32,
            )
    return total.reshape(grads.shape[0], side * side, kernel.shape[1])


def conv_same_weight(images, grads, side):
    padded = padded_grid(images, side)
    flat = flatten_rows(grads)
    terms = []
    for row in range(3):
        for column in range(3):
            window = padded[:, row : row + side, column : column + side, :].reshape(
                -1, images.shape[2]
            )
            terms.append(
                lax.dot_general(
                    window, flat, (((0,), (0,)), ((), ())), preferred_element_type=jnp.float32
                )
            )
    return jnp.stack(terms)


def conv_half_back(grads, kernel, side):
    half = side // 2
    count = grads.shape[0]
    flat = flatten_rows(grads)
    canvas = None
    for row in range(3):
        for column in range(3):
            term = lax.dot_general(
                flat,
                kernel[3 * row + column],
                (((1,), (1,)), ((), ())),
                preferred_element_type=jnp.float32,
            )
            term = term.reshape(count, half, half, kernel.shape[1])
            placed = lax.pad(
                term,
                jnp.zeros((), term.dtype),
                ((0, 0, 0), (row, 3 - row, 1), (column, 3 - column, 1), (0, 0, 0)),
            )
            canvas = placed if canvas is None else canvas + placed
    return canvas[:, 1 : side + 1, 1 : side + 1, :].reshape(count, side * side, kernel.shape[1])


def conv_half_weight(images, grads, side):
    padded = padded_grid(images, side)
    flat = flatten_rows(grads)
    terms = []
    for row in range(3):
        for column in range(3):
            window = padded[:, row : row + side : 2, column : column + side : 2, :].reshape(
                -1, images.shape[2]
            )
            terms.append(
                lax.dot_general(
                    window, flat, (((0,), (0,)), ((), ())), preferred_element_type=jnp.float32
                )
            )
    return jnp.stack(terms)


def gather_outer(shard):
    return lax.all_gather(shard, "cout", axis=2, tiled=True)


def gather_inner(shard):
    return lax.all_gather(shard, "cin", axis=2, tiled=True)


def sum_inner(partial_value):
    return lax.psum_scatter(partial_value, "cin", scatter_dimension=2, tiled=True)


def sum_outer(partial_value):
    return lax.psum_scatter(partial_value, "cout", scatter_dimension=2, tiled=True)


def shards(
    inner_features,
    block_input,
    first_kernel,
    expand_weight,
    reduce_weight,
    stride_kernel,
    output_grad,
):
    feature_block = gather_outer(inner_features)
    first_hidden = sum_inner(conv_same(feature_block, first_kernel, SIDE))
    first_act = smooth_gate(first_hidden).astype(jnp.bfloat16)
    first_block = gather_inner(first_act)
    expanded = sum_outer(project(first_block, expand_weight))
    joined_pre = block_input.astype(jnp.float32) + expanded
    joined = smooth_gate(joined_pre).astype(jnp.bfloat16)
    joined_wide = gather_outer(joined)
    joined_pair = lax.all_to_all(joined_wide, "section", split_axis=2, concat_axis=0, tiled=True)
    hidden_part = project(joined_pair, reduce_weight)
    cotangent_block = gather_outer(output_grad)
    back_part = conv_half_back(cotangent_block, stride_kernel, SIDE)
    hidden_whole = lax.psum(hidden_part, ("section", "cin"))
    second_act = smooth_gate(hidden_whole).astype(jnp.bfloat16)
    back_whole = lax.psum(back_part, ("section", "cin"))
    masked_second = (back_whole * gate_slope(hidden_whole)).astype(jnp.bfloat16)
    stride_gradient = conv_half_weight(second_act, cotangent_block, SIDE)
    reduce_gradient = outer_rows(joined_pair, masked_second)
    joined_back = project_back(masked_second, reduce_weight)
    joined_home = lax.all_to_all(joined_back, "section", split_axis=0, concat_axis=2, tiled=True)
    back_joined = sum_outer(joined_home)
    input_gradient = (back_joined * gate_slope(joined_pre)).astype(jnp.bfloat16)
    input_wide = gather_outer(input_gradient)
    expand_local = outer_rows(first_block, input_wide)
    back_first = sum_inner(project_back(input_wide, expand_weight))
    masked_first = (back_first * gate_slope(first_hidden)).astype(jnp.bfloat16)
    masked_block = gather_inner(masked_first)
    inner_gradient = sum_outer(conv_same_back(masked_block, first_kernel, SIDE))
    first_local = conv_same_weight(feature_block, masked_block, SIDE)
    first_gradient, expand_gradient = (
        lax.psum(first_local.astype(jnp.bfloat16), "section").astype(jnp.float32),
        lax.psum(expand_local.astype(jnp.bfloat16), "section").astype(jnp.float32),
    )
    return (
        inner_gradient,
        input_gradient,
        first_gradient,
        expand_gradient,
        reduce_gradient,
        stride_gradient,
    )


def solution(mesh):
    return jax.shard_map(
        shards,
        mesh=mesh,
        in_specs=(
            P("section", None, ("cin", "cout")),
            P("section", None, ("cin", "cout")),
            P(None, "cin", "cout"),
            P("cout", "cin"),
            P(("cin", "section"), "cout"),
            P(None, "cout", ("section", "cin")),
            P(None, None, ("section", "cin", "cout")),
        ),
        out_specs=(
            P("section", None, ("cin", "cout")),
            P("section", None, ("cin", "cout")),
            P(None, "cin", "cout"),
            P("cout", "cin"),
            P(("cin", "section"), "cout"),
            P(None, "cout", ("section", "cin")),
        ),
        check_vma=False,
    )
```

profile of v0, /device:TPU:0, one launch (start us, length us, event | category | flops | bytes accessed | tf_op | source)
XLA Modules:
  0.0 957.9 jit_solution(9622084547646178098)
XLA Ops:
  7.2 30.3 %all_gather.19 = bf16[1,784,320]{1,2,0:T(8,128)(2,1)S(1)} all-gather(bf16[1,784,40]{1,2,0:T(8,128)(2,1)} %param.7), channel_id=1, replica_groups=mesh['section'=2,'cin'=8,'cout'=8] {'cout'}, dimensions={2}, use_global_device_ids=true | all-gather | bytes 564480 | tf_op jit(solution)/shard_map/all_gather | solution.py:137
  68.5 28.8 %all_gather.18 = bf16[2,196,320]{1,2,0:T(8,128)(2,1)S(1)} all-gather(bf16[2,196,40]{1,2,0:T(8,128)(2,1)S(1)} %copy-done.55), channel_id=1, replica_groups=mesh['section'=2,'cin'=8,'cout'=8] {'cout'}, dimensions={2}, use_global_device_ids=true | all-gather | bytes 282240 | tf_op jit(solution)/shard_map/all_gather | solution.py:137
  102.0 16.4 %pad.56 = f32[2,28,28,640]{3,2,1,0:T(8,128)} pad(f32[2,14,14,640]{3,2,1,0:T(8,128)} %fusion.54, f32[]{:T(128)} %constant.3.clone.1), padding=0_0_0x1_0_1x1_0_1x0_0_0 | pad | bytes 5017604 | tf_op jit(solution)/shard_map/slice | solution.py:116
  118.4 11.1 %pad.55 = f32[2,28,28,640]{3,2,1,0:T(8,128)} pad(f32[2,14,14,640]{3,2,1,0:T(8,128)S(1)} %fusion.56, f32[]{:T(128)} %constant.3.clone.1), padding=0_0_0x1_0_1x0_1_1x0_0_0 | pad | bytes 5017604 | tf_op jit(solution)/shard_map/slice | solution.py:116
  131.0 11.1 %pad.53 = f32[2,28,28,640]{3,2,1,0:T(8,128)} pad(f32[2,14,14,640]{3,2,1,0:T(8,128)S(1)} %fusion.60, f32[]{:T(128)} %constant.3.clone.1), padding=0_0_0x0_1_1x1_0_1x0_0_0 | pad | bytes 5017604 | tf_op jit(solution)/shard_map/slice | solution.py:116
  143.6 11.1 %pad.52 = f32[2,28,28,640]{3,2,1,0:T(8,128)} pad(f32[2,14,14,640]{3,2,1,0:T(8,128)S(1)} %fusion.62, f32[]{:T(128)} %constant.3.clone.1), padding=0_0_0x0_1_1x0_1_1x0_0_0 | pad | bytes 5017604 | tf_op jit(solution)/shard_map/slice | solution.py:116
  156.2 11.3 %pad.41 = f32[2,30,30,640]{3,2,1,0:T(8,128)} pad(f32[2,14,14,640]{3,2,1,0:T(8,128)S(1)} %fusion.66, f32[]{:T(128)} %constant.3.clone.1), padding=0_0_0x0_3_1x2_1_1x0_0_0 | pad | bytes 5611524 | tf_op jit(solution)/shard_map/pad | solution.py:110
  168.9 11.2 %pad.39 = f32[2,30,30,640]{3,2,1,0:T(8,128)} pad(f32[2,14,14,640]{3,2,1,0:T(8,128)S(1)} %fusion.70, f32[]{:T(128)} %constant.3.clone.1), padding=0_0_0x0_3_1x0_3_1x0_0_0 | pad | bytes 5611524 | tf_op jit(solution)/shard_map/pad | solution.py:110
  181.6 11.3 %pad.40 = f32[2,30,30,640]{3,2,1,0:T(8,128)} pad(f32[2,14,14,640]{3,2,1,0:T(8,128)S(1)} %fusion.68, f32[]{:T(128)} %constant.3.clone.1), padding=0_0_0x0_3_1x1_2_1x0_0_0 | pad | bytes 5611524 | tf_op jit(solution)/shard_map/pad | solution.py:110
  194.4 11.1 %pad.74 = f32[2,28,29,640]{3,2,1,0:T(8,128)} pad(f32[2,14,14,640]{3,2,1,0:T(8,128)S(1)} %fusion.64, f32[]{:T(128)} %constant.3.clone.1), padding=0_0_0x0_1_1x0_2_1x0_0_0 | pad | bytes 5160964
  207.0 11.2 %pad.73 = f32[2,28,29,640]{3,2,1,0:T(8,128)} pad(f32[2,14,14,640]{3,2,1,0:T(8,128)S(1)} %fusion.58, f32[]{:T(128)} %constant.3.clone.1), padding=0_0_0x1_0_1x0_2_1x0_0_0 | pad | bytes 5160964
  219.1 36.6 %all_gather.20 = bf16[1,784,320]{1,2,0:T(8,128)(2,1)S(1)} all-gather(bf16[1,784,40]{1,2,0:T(8,128)(2,1)S(1)} %multiply_convert_fusion.4), channel_id=1, replica_groups=mesh['section'=2,'cin'=8,'cout'=8] {'cin'}, dimensions={2}, use_global_device_ids=true | all-gather | bytes 564480 | tf_op jit(solution)/shard_map/all_gather | solution.py:141
  257.3 4.1 copy.97
  261.8 6.8 add_add_fusion
  268.6 11.1 %fusion.4 = f32[2,28,28,640]{3,2,1,0:T(8,128)S(1)} fusion(f32[2,28,28,640]{3,2,1,0:T(8,128)} %pad.56, f32[2,28,28,640]{3,2,1,0:T(8,128)} %pad.55, f32[2,28,28,640]{3,2,1,0:T(8,128)} %pad.53, f32[2,28,28,640]{3,2,1,0:T(8,128)} %pad.52, f32[2,30,30,640]{3,2,1,0:T(8,128)S(1)} %add_add_fusion, f32[2,28,29,640]{3,2,1,0:T(8,128)} %pad.74, f32[2,28,29,640]{3,2,1,0:T(8,128)} %pad.73), kind=kLoop, calls=%fused_computation.6 | loop fusion | flops 6021120 | bytes 32112640 | tf_op jit(solution)/shard_map/add | solution.py:115
  286.3 58.8 %all-reduce.24.cloned.1.call-done = f32[1,784,640]{1,0,2:T(1,128)} async-done(((f32[1,784,640]{1,0,2:T(1,128)}), f32[1,784,640]{1,0,2:T(1,128)}) %all-reduce.24.cloned.1.call-update) | async-done | bytes 2007056
  346.9 31.0 %all_gather.21 = bf16[1,784,640]{1,2,0:T(8,128)(2,1)S(1)} all-gather(bf16[1,784,80]{1,2,0:T(8,128)(2,1)S(1)} %multiply_convert_fusion.2), channel_id=1, replica_groups=mesh['section'=2,'cin'=8,'cout'=8] {'cout'}, dimensions={2}, use_global_device_ids=true | all-gather | bytes 1128960 | tf_op jit(solution)/shard_map/all_gather | solution.py:137
  380.2 9.0 reduce
  392.2 4.7 all_to_all.33
  404.7 195.4 %all-reduce.28.cloned.1.call-done = (f32[2,784,640]{2,1,0:T(8,128)}, f32[2,784,640]{2,1,0:T(8,128)}) async-done(((f32[2,784,640]{2,1,0:T(8,128)}, f32[2,784,640]{2,1,0:T(8,128)}), (f32[2,784,640]{2,1,0:T(8,128)}, f32[2,784,640]{2,1,0:T(8,128)})) %all-reduce.28.cloned.1.call-update) | async-done | bytes 8028176 | tf_op jit(solution)/shard_map/psum | solution.py:175
  600.2 5.1 multiply_convert_fusion
  606.6 5.6 all_to_all.34
  612.2 3.7 copy.100
  616.0 83.4 %all-reduce.26.cloned.1.call-done = f32[1,784,640]{1,0,2:T(1,128)} async-done(((f32[1,784,640]{1,0,2:T(1,128)}), f32[1,784,640]{1,0,2:T(1,128)}) %all-reduce.26.cloned.1.call-update) | async-done | bytes 2007056
  700.6 30.6 %all_gather.22 = bf16[1,784,640]{1,2,0:T(8,128)(2,1)S(1)} all-gather(bf16[1,784,80]{1,2,0:T(8,128)(2,1)S(1)} %fusion.85), channel_id=1, replica_groups=mesh['section'=2,'cin'=8,'cout'=8] {'cout'}, dimensions={2}, use_global_device_ids=true | all-gather | bytes 1128960 | tf_op jit(solution)/shard_map/all_gather | solution.py:137
  736.7 3.6 reshape.211
  741.9 5.0 fusion.137
  756.3 45.9 %reduce-scatter.16.cloned.1.call-done = f32[1,784,40]{1,2,0:T(8,128)} async-done(((f32[1,784,320]{1,2,0:T(8,128)}), f32[1,784,40]{1,2,0:T(8,128)}) %reduce-scatter.16.cloned.1.call-update) | async-done | bytes 125456
  803.2 35.5 %all_gather.23 = bf16[1,784,320]{1,2,0:T(8,128)(2,1)S(1)} all-gather(bf16[1,784,40]{1,2,0:T(8,128)(2,1)S(1)} %multiply_convert_fusion.3), channel_id=1, replica_groups=mesh['section'=2,'cin'=8,'cout'=8] {'cin'}, dimensions={2}, use_global_device_ids=true | all-gather | bytes 564480 | tf_op jit(solution)/shard_map/all_gather | solution.py:141
  841.3 6.5 pad_slice_fusion.4
  906.7 4.1 convert_element_type.43
  911.7 38.9 %reduce-scatter.18.cloned.1.call-done = f32[1,784,40]{1,2,0:T(8,128)} async-done(((f32[1,784,320]{1,2,0:T(8,128)}), f32[1,784,40]{1,2,0:T(8,128)}) %reduce-scatter.18.cloned.1.call-update) | async-done | bytes 125456
  (240 shorter events, 151.7 us)
Async XLA Ops:
  7.2 394.1 %copy-start = (bf16[320,640]{1,0:T(8,128)(2,1)S(1)}, bf16[320,640]{1,0:T(8,128)(2,1)}, u32[]{:S(2)}) copy-start(bf16[320,640]{1,0:T(8,128)(2,1)} %param.11) | copy-start | bytes 1228804
  7.2 211.0 %reduce-scatter.14.cloned.1.call-start = ((), (), s32[]{:S(2)}) async-start(), calls=%async_computation.7 | async-start | bytes 1290240
  42.1 6.6 copy-start.1
  68.4 276.6 %all-reduce.24.cloned.1.call-start = ((), (), s32[]{:S(2)}) async-start(), calls=%async_computation.5 | async-start | bytes 4587520
  206.9 49.6 %copy-start.48 = (bf16[320,640]{1,0:T(8,128)(2,1)S(1)}, bf16[320,640]{1,0:T(8,128)(2,1)}, u32[]{:S(2)}) copy-start(bf16[320,640]{1,0:T(8,128)(2,1)} %param.10) | copy-start | bytes 1228804
  261.5 338.7 %all-reduce.28.cloned.1.call-start = ((), (), s32[]{:S(2)}) async-start(), calls=%async_computation.10 | async-start | bytes 16056320 | tf_op jit(solution)/shard_map/psum | solution.py:175
  282.8 63.3 %copy-start.52 = (bf16[1,784,80]{1,2,0:T(8,128)(2,1)S(1)}, bf16[1,784,80]{1,2,0:T(8,128)(2,1)}, u32[]{:S(2)}) copy-start(bf16[1,784,80]{1,2,0:T(8,128)(2,1)} %param.8) | copy-start | bytes 376324
  404.7 294.7 %all-reduce.26.cloned.1.call-start = ((), (), s32[]{:S(2)}) async-start(), calls=%async_computation.6 | async-start | bytes 4587520
  615.9 84.6 %copy-start.15 = (f32[1,784,80]{1,0,2:T(1,128)S(1)}, f32[1,784,80]{1,0,2:T(1,128)}, u32[]{:S(2)}) copy-start(f32[1,784,80]{1,0,2:T(1,128)} %copy-done.14) | copy-start | bytes 752644
  615.9 116.3 %copy-start.49 = (bf16[320,640]{1,0:T(8,128)(2,1)S(1)}, bf16[320,640]{1,0:T(8,128)(2,1)}, u32[]{:S(2)}) copy-start(bf16[320,640]{1,0:T(8,128)(2,1)} %param.10) | copy-start | bytes 1228804
  615.9 186.3 %reduce-scatter.16.cloned.1.call-start = ((), (), s32[]{:S(2)}) async-start(), calls=%async_computation.8 | async-start | bytes 1290240
  700.6 33.3 %copy-start.51 = (bf16[1,784,80]{1,2,0:T(8,128)(2,1)}, bf16[1,784,80]{1,2,0:T(8,128)(2,1)S(1)}, u32[]{:S(2)}) copy-start(bf16[1,784,80]{1,2,0:T(8,128)(2,1)S(1)} %fusion.85) | copy-start | bytes 376324
  733.9 172.8 %all-reduce.30.cloned.1.call-start = ((), (), s32[]{:S(2)}) async-start(), calls=%async_computation.11 | async-start | bytes 5242880 | tf_op jit(solution)/shard_map/psum | solution.py:191
  736.7 3.6 copy-start.5
  748.9 5.8 copy-start.10
  749.9 4.9 copy-start.36
  752.3 49.9 %copy-start.53 = (f32[1,784,40]{1,2,0:T(8,128)S(1)}, f32[1,784,40]{1,2,0:T(8,128)}, u32[]{:S(2)}) copy-start(f32[1,784,40]{1,2,0:T(8,128)} %reduce-scatter.14.cloned.1.call-done) | copy-start | bytes 376324
  754.8 84.3 %copy-start.27 = (bf16[784,320]{1,0:T(8,128)(2,1)S(1)}, bf16[784,320]{1,0:T(8,128)(2,1)}, u32[]{:S(2)}) copy-start(bf16[784,320]{1,0:T(8,128)(2,1)} %reshape.186) | copy-start | bytes 1505284
  841.3 8.6 copy-start.2
  867.7 5.2 copy-start.7
  867.7 5.2 copy-start.17
  870.3 5.0 copy-start.26
  872.9 3.7 copy-start.25
  874.1 3.7 copy-start.21
  875.3 3.8 copy-start.23
  880.4 70.2 %reduce-scatter.18.cloned.1.call-start = ((), (), s32[]{:S(2)}) async-start(), calls=%async_computation.9 | async-start | bytes 1290240
  893.2 3.7 copy-start.45
  895.6 4.1 copy-start.46
  896.9 4.1 copy-start.47
  898.3 4.1 copy-start.4
  898.3 4.1 copy-start.50
  906.7 4.1 copy-start.54
  (32 other events, 46.4 us)
Sparse Core Ops, SparseCore 0:
  68.6 69.3 reduce-scatter.13
  261.6 83.4 all-reduce.23
  404.8 195.3 all-reduce.27
  616.1 83.3 all-reduce.25
  734.0 68.1 reduce-scatter.15
  880.6 26.0 all-reduce.29
  909.6 40.9 reduce-scatter.17
where the time goes:
time: 967 us; the launch traced here: 958 us
  waiting for transfers between devices  425 us (44%)
  local copies, waits for them, and re-layouts  203 us (21%)
  blocking collectives  203 us (21%)
  matrix products  70.4 us (7%)
  other arithmetic  39.2 us (4%)
  between operations  15.9 us (2%)
    unnamed x12, waiting for transfers between devices  227 us
    psum x1, waiting for transfers between devices, shards(): back_whole = lax.psum(back_part, ('section', 'cin'))  195 us
    all_gather x4, blocking collectives, gather_outer(): return lax.all_gather(shard, 'cout', axis=2, tiled=True)  121 us
    all_gather x2, blocking collectives, gather_inner(): return lax.all_gather(shard, 'cin', axis=2, tiled=True)  72.1 us
    slice x5, local copies, waits for them, and re-layouts, conv_half_back(): canvas[:, 1:side + 1, 1:side + 1, :]  52.9 us
    unnamed x123, local copies, waits for them, and re-layouts  39.9 us
    pad x3, local copies, waits for them, and re-layouts, conv_half_back(): lax.pad(term, jnp.zeros((), term.dtype), ((0, 0, 0), (row, 3 - row, 1), (...  33.8 us
  transfers between devices with their start and end apart: 7, of which 6 were waited for; matrix products, arithmetic and copies ran while one was open for 20% of the time, Pallas kernels for 0%

commit v1 on v0

--- a/solution.py
+++ b/solution.py
@@ -134,7 +134,9 @@
 
 
 def gather_outer(shard):
-    return lax.all_gather(shard, "cout", axis=2, tiled=True)
+    return jnp.concatenate(
+        lax.all_to_all(jnp.stack([shard] * lax.axis_size("cout")), "cout", 0, 0), axis=2
+    )
 
 
 def gather_inner(shard):

time: 967 us -> 851 us (0.88)
  blocking collectives: 203 us -> 113 us
  waiting for transfers between devices: 425 us -> 387 us
    all_gather x4 -> x0, blocking collectives: 121 us -> none  [gather_outer(): return lax.all_gather(shard, 'cout', axis=2, tiled=True)]
    unnamed x12, waiting for transfers between devices: 227 us -> 181 us
    all_to_all x0 -> x2, blocking collectives: none -> 32.7 us  [gather_outer(): lax.all_to_all(jnp.stack([shard] * lax.axis_size('cout')), 'cout', 0, 0)]
    unnamed x123 -> x120, local copies, waits for them, and re-layouts: 39.9 us -> 41.3 us
  transfers between devices with their start and end apart: 7 -> 9, of which waited for: 6 -> 8; matrix products, arithmetic and copies ran while one was open for 20% -> 23% of each run, Pallas kernels for 0% -> 0%
where the time goes in v1:
time: 851 us; the launch traced here: 843 us
  waiting for transfers between devices  387 us (45%)
  local copies, waits for them, and re-layouts  209 us (25%)
  blocking collectives  113 us (13%)
  matrix products  67.1 us (8%)
  other arithmetic  43.1 us (5%)
  between operations  15.9 us (2%)
    psum x1, waiting for transfers between devices, shards(): back_whole = lax.psum(back_part, ('section', 'cin'))  197 us
    unnamed x12, waiting for transfers between devices  181 us
    all_gather x2, blocking collectives, gather_inner(): return lax.all_gather(shard, 'cin', axis=2, tiled=True)  70.6 us
    slice x5, local copies, waits for them, and re-layouts, conv_half_back(): canvas[:, 1:side + 1, 1:side + 1, :]  47.7 us
    unnamed x120, local copies, waits for them, and re-layouts  41.3 us
    pad x3, local copies, waits for them, and re-layouts, conv_half_back(): lax.pad(term, jnp.zeros((), term.dtype), ((0, 0, 0), (row, 3 - row, 1), (...  33.8 us
    all_to_all x2, blocking collectives, gather_outer(): lax.all_to_all(jnp.stack([shard] * lax.axis_size('cout')), 'cout', 0, 0)  32.7 us
    add x2, other arithmetic, conv_half_back(): canvas = placed if canvas is None else canvas + placed  21.6 us
  transfers between devices with their start and end apart: 9, of which 8 were waited for; matrix products, arithmetic and copies ran while one was open for 23% of the time, Pallas kernels for 0%

profile of v1, /device:TPU:0, one launch (start us, length us, event | category | flops | bytes accessed | tf_op | source)
XLA Modules:
  0.0 842.6 jit_solution(17133897206716523032)
XLA Ops:
  8.2 16.3 %all_to_all.53 = bf16[8,1,784,40]{2,3,1,0:T(8,128)(2,1)S(1)} all-to-all(bf16[8,1,784,40]{2,3,1,0:T(8,128)(2,1)S(1)} %stack.115), channel_id=1, replica_groups=mesh['section'=2,'cin'=8,'cout'=8] {'cout'}, dimensions={0} | all-to-all | bytes 1003520 | tf_op jit(solution)/shard_map/all_to_all | solution.py:138
  28.5 6.2 pad_slice_fusion.8
  64.5 6.2 all-to-all-done
  74.6 11.2 %pad.39 = f32[2,30,30,640]{3,2,1,0:T(8,128)} pad(f32[2,14,14,640]{3,2,1,0:T(8,128)S(1)} %fusion.66, f32[]{:T(128)} %constant.3.clone.1), padding=0_0_0x0_3_1x0_3_1x0_0_0 | pad | bytes 5611524 | tf_op jit(solution)/shard_map/pad | solution.py:110
  87.3 11.3 %pad.40 = f32[2,30,30,640]{3,2,1,0:T(8,128)} pad(f32[2,14,14,640]{3,2,1,0:T(8,128)S(1)} %fusion.64, f32[]{:T(128)} %constant.3.clone.1), padding=0_0_0x0_3_1x1_2_1x0_0_0 | pad | bytes 5611524 | tf_op jit(solution)/shard_map/pad | solution.py:110
  100.1 11.3 %pad.41 = f32[2,30,30,640]{3,2,1,0:T(8,128)} pad(f32[2,14,14,640]{3,2,1,0:T(8,128)S(1)} %fusion.62, f32[]{:T(128)} %constant.3.clone.1), padding=0_0_0x0_3_1x2_1_1x0_0_0 | pad | bytes 5611524 | tf_op jit(solution)/shard_map/pad | solution.py:110
  112.8 11.2 %pad.52 = f32[2,28,28,640]{3,2,1,0:T(8,128)} pad(f32[2,14,14,640]{3,2,1,0:T(8,128)S(1)} %fusion.58, f32[]{:T(128)} %constant.3.clone.1), padding=0_0_0x0_1_1x0_1_1x0_0_0 | pad | bytes 5017604 | tf_op jit(solution)/shard_map/slice | solution.py:116
  128.0 35.3 %all_gather.6 = bf16[1,784,320]{1,2,0:T(8,128)(2,1)S(1)} all-gather(bf16[1,784,40]{1,2,0:T(8,128)(2,1)S(1)} %multiply_convert_fusion.4), channel_id=1, replica_groups=mesh['section'=2,'cin'=8,'cout'=8] {'cin'}, dimensions={2}, use_global_device_ids=true | all-gather | bytes 564480 | tf_op jit(solution)/shard_map/all_gather | solution.py:143
  165.9 3.8 copy.100
  171.2 11.1 %pad.53 = f32[2,28,28,640]{3,2,1,0:T(8,128)} pad(f32[2,14,14,640]{3,2,1,0:T(8,128)S(1)} %fusion.56, f32[]{:T(128)} %constant.3.clone.1), padding=0_0_0x0_1_1x1_0_1x0_0_0 | pad | bytes 5017604 | tf_op jit(solution)/shard_map/slice | solution.py:116
  183.8 11.1 %pad.55 = f32[2,28,28,640]{3,2,1,0:T(8,128)} pad(f32[2,14,14,640]{3,2,1,0:T(8,128)S(1)} %fusion.52, f32[]{:T(128)} %constant.3.clone.1), padding=0_0_0x1_0_1x0_1_1x0_0_0 | pad | bytes 5017604 | tf_op jit(solution)/shard_map/slice | solution.py:116
  196.4 11.2 %pad.56 = f32[2,28,28,640]{3,2,1,0:T(8,128)} pad(f32[2,14,14,640]{3,2,1,0:T(8,128)S(1)} %fusion.50, f32[]{:T(128)} %constant.3.clone.1), padding=0_0_0x1_0_1x1_0_1x0_0_0 | pad | bytes 5017604 | tf_op jit(solution)/shard_map/slice | solution.py:116
  209.0 11.2 %pad.73 = f32[2,28,29,640]{3,2,1,0:T(8,128)} pad(f32[2,14,14,640]{3,2,1,0:T(8,128)S(1)} %fusion.54, f32[]{:T(128)} %constant.3.clone.1), padding=0_0_0x1_0_1x0_2_1x0_0_0 | pad | bytes 5160964
  221.7 11.1 %pad.74 = f32[2,28,29,640]{3,2,1,0:T(8,128)} pad(f32[2,14,14,640]{3,2,1,0:T(8,128)S(1)} %fusion.60, f32[]{:T(128)} %constant.3.clone.1), padding=0_0_0x0_1_1x0_2_1x0_0_0 | pad | bytes 5160964
  232.8 9.2 %add_add_fusion = f32[2,30,30,640]{3,2,1,0:T(8,128)} fusion(f32[2,30,30,640]{3,2,1,0:T(8,128)} %pad.41, f32[2,30,30,640]{3,2,1,0:T(8,128)} %pad.39, f32[2,30,30,640]{3,2,1,0:T(8,128)} %pad.40), kind=kLoop, calls=%fused_computation | loop fusion | flops 2304000 | bytes 18432000 | tf_op jit(solution)/shard_map/add | solution.py:115
  242.0 10.0 %all-reduce.24.cloned.1.call-done = f32[1,784,640]{1,0,2:T(1,128)} async-done(((f32[1,784,640]{1,0,2:T(1,128)}), f32[1,784,640]{1,0,2:T(1,128)}) %all-reduce.24.cloned.1.call-update) | async-done | bytes 2007056
  255.0 3.8 all-to-all-start.2
  258.8 12.4 %fusion.4 = f32[2,28,28,640]{3,2,1,0:T(8,128)S(1)} fusion(f32[2,28,28,640]{3,2,1,0:T(8,128)} %pad.56, f32[2,28,28,640]{3,2,1,0:T(8,128)} %pad.55, f32[2,28,28,640]{3,2,1,0:T(8,128)} %pad.53, f32[2,28,28,640]{3,2,1,0:T(8,128)} %pad.52, f32[2,30,30,640]{3,2,1,0:T(8,128)} %add_add_fusion, f32[2,28,29,640]{3,2,1,0:T(8,128)} %pad.74, f32[2,28,29,640]{3,2,1,0:T(8,128)} %pad.73), kind=kLoop, calls=%fused_computation.6 | loop fusion | flops 6021120 | bytes 32112640 | tf_op jit(solution)/shard_map/add | solution.py:115
  281.2 9.1 %reduce = bf16[640,784]{1,0:T(8,128)(2,1)} reduce(bf16[640,1,784]{2,1,0:T(2,128)(2,1)S(1)} %bitcast.341, bf16[]{:T(256)} %broadcast.55), dimensions={1}, to_apply=%bitcast.337.reduce_sub_computation | reduce | bytes 2007042
  293.4 4.5 all_to_all.54
  305.7 196.8 %all-reduce.28.cloned.1.call-done = (f32[2,784,640]{2,1,0:T(8,128)}, f32[2,784,640]{2,1,0:T(8,128)}) async-done(((f32[2,784,640]{2,1,0:T(8,128)}, f32[2,784,640]{2,1,0:T(8,128)}), (f32[2,784,640]{2,1,0:T(8,128)}, f32[2,784,640]{2,1,0:T(8,128)})) %all-reduce.28.cloned.1.call-update) | async-done | bytes 8028176 | tf_op jit(solution)/shard_map/psum | solution.py:177
  502.5 5.1 multiply_convert_fusion
  509.0 5.6 all_to_all.55
  518.3 83.4 %all-reduce.26.cloned.1.call-done = f32[1,784,640]{1,0,2:T(1,128)} async-done(((f32[1,784,640]{1,0,2:T(1,128)}), f32[1,784,640]{1,0,2:T(1,128)}) %all-reduce.26.cloned.1.call-update) | async-done | bytes 2007056
  603.1 16.4 %all_to_all.56 = bf16[8,1,784,80]{2,3,1,0:T(8,128)(2,1)S(1)} all-to-all(bf16[8,1,784,80]{2,3,1,0:T(8,128)(2,1)S(1)} %stack.117), channel_id=1, replica_groups=mesh['section'=2,'cin'=8,'cout'=8] {'cout'}, dimensions={0} | all-to-all | bytes 2007040 | tf_op jit(solution)/shard_map/all_to_all | solution.py:138
  624.8 3.8 reshape.228
  630.1 5.0 fusion.125
  644.5 45.4 %reduce-scatter.16.cloned.1.call-done = f32[1,784,40]{1,2,0:T(8,128)} async-done(((f32[1,784,320]{1,2,0:T(8,128)}), f32[1,784,40]{1,2,0:T(8,128)}) %reduce-scatter.16.cloned.1.call-update) | async-done | bytes 125456
  690.8 35.3 %all_gather.7 = bf16[1,784,320]{1,2,0:T(8,128)(2,1)S(1)} all-gather(bf16[1,784,40]{1,2,0:T(8,128)(2,1)S(1)} %multiply_convert_fusion.3), channel_id=1, replica_groups=mesh['section'=2,'cin'=8,'cout'=8] {'cin'}, dimensions={2}, use_global_device_ids=true | all-gather | bytes 564480 | tf_op jit(solution)/shard_map/all_gather | solution.py:143
  741.0 6.9 pad_slice_fusion.4
  791.4 4.1 convert_element_type.49
  796.5 38.9 %reduce-scatter.18.cloned.1.call-done = f32[1,784,40]{1,2,0:T(8,128)} async-done(((f32[1,784,320]{1,2,0:T(8,128)}), f32[1,784,40]{1,2,0:T(8,128)}) %reduce-scatter.18.cloned.1.call-update) | async-done | bytes 125456
  (243 shorter events, 162.6 us)
Async XLA Ops:
  7.2 295.2 %copy-start = (bf16[320,640]{1,0:T(8,128)(2,1)S(1)}, bf16[320,640]{1,0:T(8,128)(2,1)}, u32[]{:S(2)}) copy-start(bf16[320,640]{1,0:T(8,128)(2,1)} %param.11) | copy-start | bytes 1228804
  7.2 119.8 %reduce-scatter.14.cloned.1.call-start = ((), (), s32[]{:S(2)}) async-start(), calls=%async_computation.11 | async-start | bytes 1290240
  42.2 6.6 copy-start.1
  57.0 6.2 copy-start.54
  59.5 11.1 %all-to-all-start = ((bf16[8,2,196,40]{2,1,3,0:T(2,128)(2,1)}), bf16[8,2,196,40]{2,1,3,0:T(2,128)(2,1)S(1)}, u32[]{:S(2)}, u32[]{:S(2)}) async-start(bf16[8,2,196,40]{2,1,3,0:T(2,128)(2,1)} %stack.114), calls=%async_computation | async-start | bytes 655360 | tf_op jit(solution)/shard_map/all_to_all | solution.py:138
  62.9 189.0 %all-reduce.24.cloned.1.call-start = ((), (), s32[]{:S(2)}) async-start(), calls=%async_computation.9 | async-start | bytes 4587520
  232.8 21.0 %copy-start.50 = (bf16[1,784,80]{1,2,0:T(8,128)(2,1)S(1)}, bf16[1,784,80]{1,2,0:T(8,128)(2,1)}, u32[]{:S(2)}) copy-start(bf16[1,784,80]{1,2,0:T(8,128)(2,1)} %param.8) | copy-start | bytes 376324
  255.0 21.6 %all-to-all-start.2 = ((bf16[8,1,784,80]{2,3,1,0:T(8,128)(2,1)}), bf16[8,1,784,80]{2,3,1,0:T(8,128)(2,1)S(1)}, u32[]{:S(2)}, u32[]{:S(2)}) async-start(bf16[8,1,784,80]{2,3,1,0:T(8,128)(2,1)} %stack.116), calls=%async_computation.2 | async-start | bytes 2293760 | tf_op jit(solution)/shard_map/all_to_all | solution.py:138
  258.8 243.7 %all-reduce.28.cloned.1.call-start = ((), (), s32[]{:S(2)}) async-start(), calls=%async_computation.14 | async-start | bytes 16056320 | tf_op jit(solution)/shard_map/psum | solution.py:177
  305.7 296.1 %all-reduce.26.cloned.1.call-start = ((), (), s32[]{:S(2)}) async-start(), calls=%async_computation.10 | async-start | bytes 4587520
  518.3 84.6 %copy-start.15 = (f32[1,784,80]{1,0,2:T(1,128)S(1)}, f32[1,784,80]{1,0,2:T(1,128)}, u32[]{:S(2)}) copy-start(f32[1,784,80]{1,0,2:T(1,128)} %copy-done.14) | copy-start | bytes 752644
  518.3 171.6 %reduce-scatter.16.cloned.1.call-start = ((), (), s32[]{:S(2)}) async-start(), calls=%async_computation.12 | async-start | bytes 1290240
  602.8 17.8 %copy-start.47 = (bf16[320,640]{1,0:T(8,128)(2,1)S(1)}, bf16[320,640]{1,0:T(8,128)(2,1)}, u32[]{:S(2)}) copy-start(bf16[320,640]{1,0:T(8,128)(2,1)} %param.10) | copy-start | bytes 1228804
  603.0 16.5 %copy-start.49 = (bf16[1,784,80]{1,2,0:T(8,128)(2,1)}, bf16[1,784,80]{1,2,0:T(8,128)(2,1)S(1)}, u32[]{:S(2)}) copy-start(bf16[1,784,80]{1,2,0:T(8,128)(2,1)S(1)} %fusion.81) | copy-start | bytes 376324
  622.3 169.1 %all-reduce.30.cloned.1.call-start = ((), (), s32[]{:S(2)}) async-start(), calls=%async_computation.15 | async-start | bytes 5242880 | tf_op jit(solution)/shard_map/psum | solution.py:193
  624.7 3.8 copy-start.5
  637.2 5.8 copy-start.10
  638.2 4.8 copy-start.35
  640.6 49.3 %copy-start.51 = (f32[1,784,40]{1,2,0:T(8,128)S(1)}, f32[1,784,40]{1,2,0:T(8,128)}, u32[]{:S(2)}) copy-start(f32[1,784,40]{1,2,0:T(8,128)} %reduce-scatter.14.cloned.1.call-done) | copy-start | bytes 376324
  640.6 85.5 %copy-start.28 = (bf16[784,320]{1,0:T(8,128)(2,1)S(1)}, bf16[784,320]{1,0:T(8,128)(2,1)}, u32[]{:S(2)}) copy-start(bf16[784,320]{1,0:T(8,128)(2,1)} %reshape.201) | copy-start | bytes 1505284
  726.1 12.6 %copy-start.6 = (bf16[1,784,320]{1,2,0:T(8,128)(2,1)}, bf16[1,784,320]{1,2,0:T(8,128)(2,1)S(1)}, u32[]{:S(2)}) copy-start(bf16[1,784,320]{1,2,0:T(8,128)(2,1)S(1)} %all_gather.7) | copy-start | bytes 1505284
  727.4 5.1 copy-start.25
  730.0 4.9 copy-start.23
  732.4 3.7 copy-start.21
  734.9 3.8 copy-start.19
  741.0 8.3 copy-start.2
  765.2 70.1 %reduce-scatter.18.cloned.1.call-start = ((), (), s32[]{:S(2)}) async-start(), calls=%async_computation.13 | async-start | bytes 1290240
  779.9 4.0 copy-start.45
  781.3 4.0 copy-start.46
  782.6 4.0 copy-start.4
  782.6 4.0 copy-start.48
  791.4 4.1 copy-start.52
  (32 other events, 50.7 us)
Sparse Core Ops, SparseCore 0:
  58.7 68.2 reduce-scatter.13
  169.8 82.0 all-reduce.23
  305.8 196.6 all-reduce.27
  518.4 83.3 all-reduce.25
  622.4 67.4 reduce-scatter.15
  765.3 26.0 all-reduce.29
  794.4 40.9 reduce-scatter.17
